TPU v7x, 32 devices: a whole 2x2x4 slice. The times are simulated.
32 devices in a mesh: dp: 8 (over z, x), table: 4 (over y, core).
Axes of the slice: x: 2, y: 2, z: 4, core: 2. Of those that a mesh axis runs over, the one named last changes fastest.
Arguments:
- feature_high: int32 [20, 2048], P(None, 'dp'), may hold values from 0 to 2047
- feature_low: int32 [20, 2048], P(None, 'dp'), may hold values from 0 to 2047
- labels: int32 [2048], P('dp'), may hold values 0 or 1
- weights: float32 [4194304], P(('dp', 'table')), may hold values from -0.6 to 0.6
- history_steps: float32 [8, 4194304], P(None, ('dp', 'table')), may hold values from -46 to 46
- history_diffs: float32 [8, 4194304], P(None, ('dp', 'table')), may hold values from -198 to 198, as said below
Outputs:
- direction: float32 [4194304], P(('dp', 'table'))
Inputs may be any that keep to these rules, and one draw needn't show every extreme that they name: Each entry of history_diffs has the sign of the matching entry of history_steps and 0.2 to 4.3 times its magnitude.
All inputs are finite; a program needn't handle non-finite values. No bound on the sum of `labels` on one device may be relied on, other than what follows from the above.
Results may differ from a plain program's by a relative error of at most 0.0001.
Values sent between devices are 32-bit elements; how exact they have to be, the bound alone decides.
A program may use at most 64 MiB of HBM per device.

v0:
```python
import jax
import jax.numpy as jnp
from jax import lax
from jax.sharding import PartitionSpec as P

TABLE = 4194304
HASHES = 4
high_mult = (40503, 96469, 255361, 362443)
low_mult = (2053, 6151, 12289, 98317)
slot_mult = (1543, 3079, 769, 3457)
shifts = (0, 1048573, 2097143, 3145727)
l2_weight = 1.0


def hashed(feature_high, feature_low, number):
    slot_index = jnp.arange(feature_high.shape[0], dtype=jnp.int32)[:, None]
    part_high = feature_high * high_mult[number] % TABLE
    part_low = feature_low * low_mult[number] % TABLE
    return (part_high + part_low + slot_index * slot_mult[number] + shifts[number]) % TABLE


def local(feature_high, feature_low, labels, weights, history_steps, history_diffs):
    width = weights.shape[0]
    shard_count = lax.axis_size("table")
    column = lax.axis_index("table")
    gathered = lax.all_gather(weights, "dp", axis=0, tiled=True)
    margin = jnp.zeros((feature_high.shape[1],), jnp.float32)
    owned_list = []
    position_list = []
    for number in range(HASHES):
        indices = hashed(feature_high, feature_low, number)
        blocks = indices // width
        owned = blocks % shard_count == column
        position = blocks // shard_count * width + indices % width
        owned_list.append(owned)
        position_list.append(position)
        margin = margin + jnp.sum(jnp.where(owned, gathered[position], 0.0), axis=0)
    margin = lax.psum(margin, "table")
    residual = jax.nn.sigmoid(margin) - labels.astype(jnp.float32)
    all_positions = jnp.concatenate([place.reshape(-1) for place in position_list])
    all_terms = jnp.concatenate(
        [jnp.where(owned, residual[None, :], 0.0).reshape(-1) for owned in owned_list]
    )
    partial_grad = jnp.zeros(gathered.shape, jnp.float32).at[all_positions].add(all_terms)
    summed = lax.psum(partial_grad, "dp")
    mine = lax.dynamic_slice_in_dim(summed, lax.axis_index("dp") * width, width)
    gradient = mine + l2_weight * weights
    memory = history_steps.shape[0]
    newest = memory - 1
    pair_sums, newest_square = lax.psum(
        (
            jnp.sum(history_steps * history_diffs, axis=1),
            jnp.sum(history_diffs[newest] * history_diffs[newest]),
        ),
        ("dp", "table"),
    )
    inverse = 1.0 / pair_sums
    current = gradient
    alphas = [None] * memory
    for which in reversed(range(memory)):
        alphas[which] = inverse[which] * lax.psum(
            jnp.sum(history_steps[which] * current), ("dp", "table")
        )
        current = current - alphas[which] * history_diffs[which]
    current = pair_sums[newest] / newest_square * current
    for which in range(memory):
        correction = inverse[which] * lax.psum(
            jnp.sum(history_diffs[which] * current), ("dp", "table")
        )
        current = current + (alphas[which] - correction) * history_steps[which]
    return -current


def solution(mesh):
    placed = (
        P(None, "dp"),
        P(None, "dp"),
        P("dp"),
        P(("dp", "table")),
        P(None, ("dp", "table")),
        P(None, ("dp", "table")),
    )
    return jax.shard_map(
        local, mesh=mesh, in_specs=placed, out_specs=P(("dp", "table")), check_vma=False
    )
```

profile of v0, /device:TPU:0, one launch (start us, length us, event | category | flops | bytes accessed | tf_op | source)
XLA Modules:
  0.0 1326.4 jit_solution(4070910795745092147)
XLA Ops:
  8.8 76.8 %all-gather.2.cloned.1.call-done = f32[1048576]{0:T(1024)} async-done(((f32[131072]{0:T(1024)}), f32[1048576]{0:T(1024)}) %all-gather.2.cloned.1.call-update) | async-done | bytes 4194320 | tf_op jit(solution)/shard_map/all_gather | solution.py:26
  85.6 60.4 %gather_fusion.3 = f32[5120]{0:T(1024)S(1)} fusion(f32[1048576]{0:T(1024)} %all-gather.2.cloned.1.call-done, s32[5120]{0:T(1024)S(1)} %broadcast_clamp_fusion), kind=kCustom, calls=%fused_computation.3 | custom fusion | bytes 61440 | tf_op jit(solution)/shard_map/gather | solution.py:37
  146.0 60.4 %gather_fusion.1 = f32[5120]{0:T(1024)S(1)} fusion(f32[1048576]{0:T(1024)} %all-gather.2.cloned.1.call-done, s32[5120]{0:T(1024)S(1)} %broadcast_clamp_fusion.2), kind=kCustom, calls=%fused_computation.1 | custom fusion | bytes 61440 | tf_op jit(solution)/shard_map/gather | solution.py:37
  206.5 60.4 %gather_fusion = f32[5120]{0:T(1024)S(1)} fusion(f32[1048576]{0:T(1024)} %all-gather.2.cloned.1.call-done, s32[5120]{0:T(1024)S(1)} %broadcast_clamp_fusion.3), kind=kCustom, calls=%fused_computation | custom fusion | bytes 61440 | tf_op jit(solution)/shard_map/gather | solution.py:37
  266.9 60.4 %gather_fusion.2 = f32[5120]{0:T(1024)S(1)} fusion(f32[1048576]{0:T(1024)} %all-gather.2.cloned.1.call-done, s32[5120]{0:T(1024)S(1)} %broadcast_clamp_fusion.1), kind=kCustom, calls=%fused_computation.2 | custom fusion | bytes 61440 | tf_op jit(solution)/shard_map/gather | solution.py:37
  333.3 109.3 %scatter_custom_fusion = f32[1048576]{0:T(1024)} fusion(s32[20480]{0:T(1024)S(1)} %bitcast.84, f32[20480]{0:T(1024)S(1)} %pad_maximum_fusion, f32[]{:T(128)} %constant.207.clone.1), kind=kCustom, calls=%fused_computation.6 | custom fusion | flops 20480 | bytes 4194308 | tf_op jit(solution)/shard_map/scatter-add | solution.py:44
  463.9 133.7 %all-reduce.4.cloned.1.call-done = f32[1048576]{0:T(1024)} async-done(((f32[1048576]{0:T(1024)}), f32[1048576]{0:T(1024)}) %all-reduce.4.cloned.1.call-update) | async-done | bytes 4194320 | tf_op jit(solution)/shard_map/psum | solution.py:45
  599.4 16.6 %fusion.61 = (f32[1,131072]{1,0:T(1,128)}, f32[1,131072]{1,0:T(1,128)S(1)}, f32[1,131072]{1,0:T(1,128)}, f32[1,131072]{1,0:T(1,128)S(1)}, f32[1,131072]{1,0:T(1,...) fusion(f32[8,131072]{1,0:T(8,128)} %param.11), kind=kLoop, calls=%fused_computation.206 | loop fusion | bytes 8388608 | tf_op jit(solution)/shard_map/slice | solution.py:64
  616.0 39.4 %all-reduce.1 = (f32[8]{0:T(128)S(1)}, f32[]{:T(128)}) all-reduce(f32[8]{0:T(128)S(1)} %multiply_reduce_fusion, f32[]{:T(128)} %multiply_reduce_fusion.16), channel_id=1, replica_groups=mesh['dp'=8,'table'=4] {'dp','table'}, use_global_device_ids=true, to_apply=%region_1.2 | all-reduce | flops 9 | bytes 72 | tf_op jit(solution)/shard_map/psum | solution.py:50
  660.4 40.3 %psum.145 = f32[]{:T(128)} all-reduce(f32[]{:T(128)} %get-tuple-element.23), channel_id=1, replica_groups=mesh['dp'=8,'table'=4] {'dp','table'}, use_global_device_ids=true, to_apply=%region_14.15 | all-reduce | flops 1 | bytes 8 | tf_op jit(solution)/shard_map/psum | solution.py:61
  703.8 40.7 %psum.146 = f32[]{:T(128)} all-reduce(f32[]{:T(128)} %multiply_reduce_fusion.14), channel_id=1, replica_groups=mesh['dp'=8,'table'=4] {'dp','table'}, use_global_device_ids=true, to_apply=%region_16.17 | all-reduce | flops 1 | bytes 8 | tf_op jit(solution)/shard_map/psum | solution.py:61
  748.7 40.4 %psum.147 = f32[]{:T(128)} all-reduce(f32[]{:T(128)} %get-tuple-element.21), channel_id=1, replica_groups=mesh['dp'=8,'table'=4] {'dp','table'}, use_global_device_ids=true, to_apply=%region_18.19 | all-reduce | flops 1 | bytes 8 | tf_op jit(solution)/shard_map/psum | solution.py:61
  792.3 40.6 %psum.148 = f32[]{:T(128)} all-reduce(f32[]{:T(128)} %multiply_reduce_fusion.12), channel_id=1, replica_groups=mesh['dp'=8,'table'=4] {'dp','table'}, use_global_device_ids=true, to_apply=%region_20.21 | all-reduce | flops 1 | bytes 8 | tf_op jit(solution)/shard_map/psum | solution.py:61
  837.1 40.3 %psum.149 = f32[]{:T(128)} all-reduce(f32[]{:T(128)} %get-tuple-element.19), channel_id=1, replica_groups=mesh['dp'=8,'table'=4] {'dp','table'}, use_global_device_ids=true, to_apply=%region_22.23 | all-reduce | flops 1 | bytes 8 | tf_op jit(solution)/shard_map/psum | solution.py:61
  881.2 40.6 %psum.150 = f32[]{:T(128)} all-reduce(f32[]{:T(128)} %multiply_reduce_fusion.10), channel_id=1, replica_groups=mesh['dp'=8,'table'=4] {'dp','table'}, use_global_device_ids=true, to_apply=%region_24.25 | all-reduce | flops 1 | bytes 8 | tf_op jit(solution)/shard_map/psum | solution.py:61
  926.0 40.2 %all-reduce = (f32[]{:T(128)}, f32[]{:T(128)}) all-reduce(f32[]{:T(128)} %get-tuple-element.17, f32[]{:T(128)} %get-tuple-element.61), channel_id=1, replica_groups=mesh['dp'=8,'table'=4] {'dp','table'}, use_global_device_ids=true, to_apply=%region_26.27 | all-reduce | flops 2 | bytes 16 | tf_op jit(solution)/shard_map/psum | solution.py:61
  970.7 40.6 %psum.152 = f32[]{:T(128)} all-reduce(f32[]{:T(128)} %multiply_reduce_fusion.8), channel_id=1, replica_groups=mesh['dp'=8,'table'=4] {'dp','table'}, use_global_device_ids=true, to_apply=%region_28.29 | all-reduce | flops 1 | bytes 8 | tf_op jit(solution)/shard_map/psum | solution.py:67
  1015.6 40.1 %psum.153 = f32[]{:T(128)} all-reduce(f32[]{:T(128)} %get-tuple-element.15), channel_id=1, replica_groups=mesh['dp'=8,'table'=4] {'dp','table'}, use_global_device_ids=true, to_apply=%region_30.31 | all-reduce | flops 1 | bytes 8 | tf_op jit(solution)/shard_map/psum | solution.py:67
  1058.8 40.7 %psum.154 = f32[]{:T(128)} all-reduce(f32[]{:T(128)} %multiply_reduce_fusion.6), channel_id=1, replica_groups=mesh['dp'=8,'table'=4] {'dp','table'}, use_global_device_ids=true, to_apply=%region_32.33 | all-reduce | flops 1 | bytes 8 | tf_op jit(solution)/shard_map/psum | solution.py:67
  1103.7 40.1 %psum.155 = f32[]{:T(128)} all-reduce(f32[]{:T(128)} %get-tuple-element.13), channel_id=1, replica_groups=mesh['dp'=8,'table'=4] {'dp','table'}, use_global_device_ids=true, to_apply=%region_34.35 | all-reduce | flops 1 | bytes 8 | tf_op jit(solution)/shard_map/psum | solution.py:67
  1147.2 40.7 %psum.156 = f32[]{:T(128)} all-reduce(f32[]{:T(128)} %multiply_reduce_fusion.4), channel_id=1, replica_groups=mesh['dp'=8,'table'=4] {'dp','table'}, use_global_device_ids=true, to_apply=%region_36.37 | all-reduce | flops 1 | bytes 8 | tf_op jit(solution)/shard_map/psum | solution.py:67
  1191.4 40.2 %psum.157 = f32[]{:T(128)} all-reduce(f32[]{:T(128)} %get-tuple-element.11), channel_id=1, replica_groups=mesh['dp'=8,'table'=4] {'dp','table'}, use_global_device_ids=true, to_apply=%region_38.39 | all-reduce | flops 1 | bytes 8 | tf_op jit(solution)/shard_map/psum | solution.py:67
  1233.7 40.6 %psum.158 = f32[]{:T(128)} all-reduce(f32[]{:T(128)} %multiply_reduce_fusion.2), channel_id=1, replica_groups=mesh['dp'=8,'table'=4] {'dp','table'}, use_global_device_ids=true, to_apply=%region_40.41 | all-reduce | flops 1 | bytes 8 | tf_op jit(solution)/shard_map/psum | solution.py:67
  1277.3 40.1 %psum.159 = f32[]{:T(128)} all-reduce(f32[]{:T(128)} %get-tuple-element.9), channel_id=1, replica_groups=mesh['dp'=8,'table'=4] {'dp','table'}, use_global_device_ids=true, to_apply=%region_42.43 | all-reduce | flops 1 | bytes 8 | tf_op jit(solution)/shard_map/psum | solution.py:67
  (73 shorter events, 67.1 us)
Async XLA Ops:
  6.5 79.1 %all-gather.2.cloned.1.call-start = ((), (), s32[]{:S(2)}) async-start(), calls=%async_computation | async-start | bytes 4718592 | tf_op jit(solution)/shard_map/all_gather | solution.py:26
  7.3 590.4 %all-reduce.4.cloned.1.call-start = ((), (), s32[]{:S(2)}) async-start(), calls=%async_computation.1 | async-start | bytes 8388608 | tf_op jit(solution)/shard_map/psum | solution.py:45
  266.9 66.3 %copy-start.4 = (s32[256]{0:T(256)S(1)}, s32[256]{0:T(256)}, u32[]{:S(2)}) copy-start(s32[256]{0:T(256)} %param.8) | copy-start | bytes 3076
  459.1 138.6 %copy-start = (f32[1,131072]{1,0:T(1,128)}, f32[1,131072]{1,0:T(1,128)S(1)}, u32[]{:S(2)}) copy-start(f32[1,131072]{1,0:T(1,128)S(1)} %get-tuple-element.59) | copy-start | bytes 1572868
  459.1 138.6 %copy-start.3 = (f32[131072]{0:T(1024)S(1)}, f32[131072]{0:T(1024)}, u32[]{:S(2)}) copy-start(f32[131072]{0:T(1024)} %param.9) | copy-start | bytes 1572868
  1100.8 174.7 %copy-start.2 = (f32[1,131072]{1,0:T(1,128)S(1)}, f32[1,131072]{1,0:T(1,128)}, u32[]{:S(2)}) copy-start(f32[1,131072]{1,0:T(1,128)} %get-tuple-element.58) | copy-start | bytes 1572868
  1145.3 173.4 %copy-start.1 = (f32[1,131072]{1,0:T(1,128)S(1)}, f32[1,131072]{1,0:T(1,128)}, u32[]{:S(2)}) copy-start(f32[1,131072]{1,0:T(1,128)} %copy-done) | copy-start | bytes 1572868
Sparse Core Ops, SparseCore 0:
  9.5 76.0 all-gather.1
  442.8 154.8 all-reduce.3
where the time goes:
time: 1340 us; the launch traced here: 1330 us
  blocking collectives  651 us (49%)
  local copies, waits for them, and re-layouts  276 us (21%)
  waiting for transfers between devices  211 us (16%)
  other arithmetic  152 us (11%)
  between operations  35.7 us (3%)
    psum x8, blocking collectives, local(): lax.psum(jnp.sum(history_diffs[which] * current), ('dp', 'table'))  323 us
    psum x7, blocking collectives, local(): lax.psum(jnp.sum(history_steps[which] * current), ('dp', 'table'))  283 us
    gather x8, local copies, waits for them, and re-layouts, local(): margin = margin + jnp.sum(jnp.where(owned, gathered[position], 0.0), axis=0)  242 us
    psum x1, waiting for transfers between devices, local(): summed = lax.psum(partial_grad, 'dp')  134 us
    scatter-add x1, other arithmetic, local(): jnp.zeros(gathered.shape, jnp.float32).at[all_positions].add(all_terms)  109 us
    all_gather x1, waiting for transfers between devices, local(): gathered = lax.all_gather(weights, 'dp', axis=0, tiled=True)  76.8 us
    psum x1, blocking collectives, local(): lax.psum((jnp.sum(history_steps * history_diffs, axis=1), jnp.sum(history...  39.4 us
  transfers between devices with their start and end apart: 2, of which 2 were waited for; matrix products, arithmetic and copies ran while one was open for 2% of the time, Pallas kernels for 0%

commit v1 on v0

--- a/solution.py
+++ b/solution.py
@@ -10,6 +10,11 @@
 slot_mult = (1543, 3079, 769, 3457)
 shifts = (0, 1048573, 2097143, 3145727)
 l2_weight = 1.0
+
+
+def axis_by_axis(array, inner_axis, outer_axis):
+    half = lax.psum(array, inner_axis)
+    return lax.psum(half, outer_axis)
 
 
 def hashed(feature_high, feature_low, number):
@@ -47,12 +52,13 @@
     gradient = mine + l2_weight * weights
     memory = history_steps.shape[0]
     newest = memory - 1
-    pair_sums, newest_square = lax.psum(
+    pair_sums, newest_square = axis_by_axis(
         (
             jnp.sum(history_steps * history_diffs, axis=1),
             jnp.sum(history_diffs[newest] * history_diffs[newest]),
         ),
-        ("dp", "table"),
+        "table",
+        "dp",
     )
     inverse = 1.0 / pair_sums
     current = gradient

time: 1340 us -> 1320 us (0.985)
  waiting for transfers between devices: 211 us -> 174 us
  blocking collectives: 651 us -> 674 us
    psum x7 -> x8, blocking collectives: 283 us -> 323 us  [local(): lax.psum(jnp.sum(history_steps[which] * current), ('dp', 'table'))]
    all_gather x1, waiting for transfers between devices: 76.8 us -> 55.7 us  [local(): gathered = lax.all_gather(weights, 'dp', axis=0, tiled=True)]
    psum x2, blocking collectives: 45.1 us -> 27.8 us  [the longest x1 21.6 us: axis_by_axis(): return lax.psum(half, outer_axis)]
    psum x1, waiting for transfers between devices: 134 us -> 117 us  [local(): summed = lax.psum(partial_grad, 'dp')]
  transfers between devices with their start and end apart: 2 -> 2, of which waited for: 2 -> 2; matrix products, arithmetic and copies ran while one was open for 2% -> 3% of each run, Pallas kernels for 0% -> 0%
where the time goes in v1:
time: 1320 us; the launch traced here: 1310 us
  blocking collectives  674 us (51%)
  local copies, waits for them, and re-layouts  276 us (21%)
  waiting for transfers between devices  174 us (13%)
  other arithmetic  152 us (12%)
  between operations  35.4 us (3%)
    psum x8, blocking collectives, local(): lax.psum(jnp.sum(history_diffs[which] * current), ('dp', 'table'))  323 us
    psum x8, blocking collectives, local(): lax.psum(jnp.sum(history_steps[which] * current), ('dp', 'table'))  323 us
    gather x8, local copies, waits for them, and re-layouts, local(): margin = margin + jnp.sum(jnp.where(owned, gathered[position], 0.0), axis=0)  242 us
    psum x1, waiting for transfers between devices, local(): summed = lax.psum(partial_grad, 'dp')  117 us
    scatter-add x1, other arithmetic, local(): jnp.zeros(gathered.shape, jnp.float32).at[all_positions].add(all_terms)  109 us
    all_gather x1, waiting for transfers between devices, local(): gathered = lax.all_gather(weights, 'dp', axis=0, tiled=True)  55.7 us
  transfers between devices with their start and end apart: 2, of which 2 were waited for; matrix products, arithmetic and copies ran while one was open for 3% of the time, Pallas kernels for 0%

profile of v1, /device:TPU:0, one launch (start us, length us, event | category | flops | bytes accessed | tf_op | source)
XLA Modules:
  0.0 1311.4 jit_solution(15483540241528861007)
XLA Ops:
  30.0 55.7 %all-gather.2.cloned.1.call-done = f32[1048576]{0:T(1024)} async-done(((f32[131072]{0:T(1024)}), f32[1048576]{0:T(1024)}) %all-gather.2.cloned.1.call-update) | async-done | bytes 4194320 | tf_op jit(solution)/shard_map/all_gather | solution.py:31
  85.6 60.4 %gather_fusion = f32[5120]{0:T(1024)S(1)} fusion(f32[1048576]{0:T(1024)} %all-gather.2.cloned.1.call-done, s32[5120]{0:T(1024)S(1)} %broadcast_clamp_fusion.3), kind=kCustom, calls=%fused_computation | custom fusion | bytes 61440 | tf_op jit(solution)/shard_map/gather | solution.py:42
  146.0 60.4 %gather_fusion.1 = f32[5120]{0:T(1024)S(1)} fusion(f32[1048576]{0:T(1024)} %all-gather.2.cloned.1.call-done, s32[5120]{0:T(1024)S(1)} %broadcast_clamp_fusion.2), kind=kCustom, calls=%fused_computation.1 | custom fusion | bytes 61440 | tf_op jit(solution)/shard_map/gather | solution.py:42
  206.5 60.4 %gather_fusion.2 = f32[5120]{0:T(1024)S(1)} fusion(f32[1048576]{0:T(1024)} %all-gather.2.cloned.1.call-done, s32[5120]{0:T(1024)S(1)} %broadcast_clamp_fusion.1), kind=kCustom, calls=%fused_computation.2 | custom fusion | bytes 61440 | tf_op jit(solution)/shard_map/gather | solution.py:42
  266.9 60.4 %gather_fusion.3 = f32[5120]{0:T(1024)S(1)} fusion(f32[1048576]{0:T(1024)} %all-gather.2.cloned.1.call-done, s32[5120]{0:T(1024)S(1)} %broadcast_clamp_fusion), kind=kCustom, calls=%fused_computation.3 | custom fusion | bytes 61440 | tf_op jit(solution)/shard_map/gather | solution.py:42
  333.9 109.3 %scatter_custom_fusion = f32[1048576]{0:T(1024)} fusion(s32[20480]{0:T(1024)S(1)} %bitcast.85, f32[20480]{0:T(1024)S(1)} %pad_maximum_fusion, f32[]{:T(128)} %constant.207.clone.1), kind=kCustom, calls=%fused_computation.6 | custom fusion | flops 20480 | bytes 4194308 | tf_op jit(solution)/shard_map/scatter-add | solution.py:49
  459.7 21.6 %all-reduce = (f32[8]{0:T(128)S(1)}, f32[]{:T(128)}) all-reduce(f32[8]{0:T(128)S(1)} %get-tuple-element.7, f32[]{:T(128)} %get-tuple-element.8), channel_id=1, replica_groups=mesh['dp'=8,'table'=4] {'dp'}, use_global_device_ids=true, to_apply=%region_2.3 | all-reduce | flops 9 | bytes 72 | tf_op jit(solution)/shard_map/psum | solution.py:17
  481.4 117.2 %all-reduce.4.cloned.1.call-done = f32[1048576]{0:T(1024)} async-done(((f32[1048576]{0:T(1024)}), f32[1048576]{0:T(1024)}) %all-reduce.4.cloned.1.call-update) | async-done | bytes 4194320 | tf_op jit(solution)/shard_map/psum | solution.py:50
  601.3 39.4 %psum.160 = f32[]{:T(128)} all-reduce(f32[]{:T(128)} %multiply_reduce_fusion.16), channel_id=1, replica_groups=mesh['dp'=8,'table'=4] {'dp','table'}, use_global_device_ids=true, to_apply=%region_14.15 | all-reduce | flops 1 | bytes 8 | tf_op jit(solution)/shard_map/psum | solution.py:67
  644.8 40.4 %psum.161 = f32[]{:T(128)} all-reduce(f32[]{:T(128)} %get-tuple-element.24), channel_id=1, replica_groups=mesh['dp'=8,'table'=4] {'dp','table'}, use_global_device_ids=true, to_apply=%region_16.17 | all-reduce | flops 1 | bytes 8 | tf_op jit(solution)/shard_map/psum | solution.py:67
  688.4 40.7 %psum.162 = f32[]{:T(128)} all-reduce(f32[]{:T(128)} %multiply_reduce_fusion.14), channel_id=1, replica_groups=mesh['dp'=8,'table'=4] {'dp','table'}, use_global_device_ids=true, to_apply=%region_18.19 | all-reduce | flops 1 | bytes 8 | tf_op jit(solution)/shard_map/psum | solution.py:67
  733.4 40.4 %psum.163 = f32[]{:T(128)} all-reduce(f32[]{:T(128)} %get-tuple-element.22), channel_id=1, replica_groups=mesh['dp'=8,'table'=4] {'dp','table'}, use_global_device_ids=true, to_apply=%region_20.21 | all-reduce | flops 1 | bytes 8 | tf_op jit(solution)/shard_map/psum | solution.py:67
  777.4 40.5 %psum.164 = f32[]{:T(128)} all-reduce(f32[]{:T(128)} %multiply_reduce_fusion.12), channel_id=1, replica_groups=mesh['dp'=8,'table'=4] {'dp','table'}, use_global_device_ids=true, to_apply=%region_22.23 | all-reduce | flops 1 | bytes 8 | tf_op jit(solution)/shard_map/psum | solution.py:67
  822.2 40.4 %psum.165 = f32[]{:T(128)} all-reduce(f32[]{:T(128)} %get-tuple-element.20), channel_id=1, replica_groups=mesh['dp'=8,'table'=4] {'dp','table'}, use_global_device_ids=true, to_apply=%region_24.25 | all-reduce | flops 1 | bytes 8 | tf_op jit(solution)/shard_map/psum | solution.py:67
  867.1 40.6 %psum.166 = f32[]{:T(128)} all-reduce(f32[]{:T(128)} %multiply_reduce_fusion.10), channel_id=1, replica_groups=mesh['dp'=8,'table'=4] {'dp','table'}, use_global_device_ids=true, to_apply=%region_26.27 | all-reduce | flops 1 | bytes 8 | tf_op jit(solution)/shard_map/psum | solution.py:67
  912.0 40.3 %psum.167 = f32[]{:T(128)} all-reduce(f32[]{:T(128)} %get-tuple-element.18), channel_id=1, replica_groups=mesh['dp'=8,'table'=4] {'dp','table'}, use_global_device_ids=true, to_apply=%region_28.29 | all-reduce | flops 1 | bytes 8 | tf_op jit(solution)/shard_map/psum | solution.py:67
  955.6 40.7 %psum.168 = f32[]{:T(128)} all-reduce(f32[]{:T(128)} %multiply_reduce_fusion.8), channel_id=1, replica_groups=mesh['dp'=8,'table'=4] {'dp','table'}, use_global_device_ids=true, to_apply=%region_30.31 | all-reduce | flops 1 | bytes 8 | tf_op jit(solution)/shard_map/psum | solution.py:73
  1000.7 40.3 %psum.169 = f32[]{:T(128)} all-reduce(f32[]{:T(128)} %get-tuple-element.16), channel_id=1, replica_groups=mesh['dp'=8,'table'=4] {'dp','table'}, use_global_device_ids=true, to_apply=%region_32.33 | all-reduce | flops 1 | bytes 8 | tf_op jit(solution)/shard_map/psum | solution.py:73
  1044.3 40.6 %psum.170 = f32[]{:T(128)} all-reduce(f32[]{:T(128)} %multiply_reduce_fusion.6), channel_id=1, replica_groups=mesh['dp'=8,'table'=4] {'dp','table'}, use_global_device_ids=true, to_apply=%region_34.35 | all-reduce | flops 1 | bytes 8 | tf_op jit(solution)/shard_map/psum | solution.py:73
  1089.1 40.2 %psum.171 = f32[]{:T(128)} all-reduce(f32[]{:T(128)} %get-tuple-element.14), channel_id=1, replica_groups=mesh['dp'=8,'table'=4] {'dp','table'}, use_global_device_ids=true, to_apply=%region_36.37 | all-reduce | flops 1 | bytes 8 | tf_op jit(solution)/shard_map/psum | solution.py:73
  1132.5 40.6 %psum.172 = f32[]{:T(128)} all-reduce(f32[]{:T(128)} %multiply_reduce_fusion.4), channel_id=1, replica_groups=mesh['dp'=8,'table'=4] {'dp','table'}, use_global_device_ids=true, to_apply=%region_38.39 | all-reduce | flops 1 | bytes 8 | tf_op jit(solution)/shard_map/psum | solution.py:73
  1176.4 40.2 %psum.173 = f32[]{:T(128)} all-reduce(f32[]{:T(128)} %get-tuple-element.12), channel_id=1, replica_groups=mesh['dp'=8,'table'=4] {'dp','table'}, use_global_device_ids=true, to_apply=%region_40.41 | all-reduce | flops 1 | bytes 8 | tf_op jit(solution)/shard_map/psum | solution.py:73
  1218.6 40.5 %psum.174 = f32[]{:T(128)} all-reduce(f32[]{:T(128)} %multiply_reduce_fusion.2), channel_id=1, replica_groups=mesh['dp'=8,'table'=4] {'dp','table'}, use_global_device_ids=true, to_apply=%region_42.43 | all-reduce | flops 1 | bytes 8 | tf_op jit(solution)/shard_map/psum | solution.py:73
  1262.3 40.2 %psum.175 = f32[]{:T(128)} all-reduce(f32[]{:T(128)} %get-tuple-element.10), channel_id=1, replica_groups=mesh['dp'=8,'table'=4] {'dp','table'}, use_global_device_ids=true, to_apply=%region_44.45 | all-reduce | flops 1 | bytes 8 | tf_op jit(solution)/shard_map/psum | solution.py:73
  (73 shorter events, 84.6 us)
Async XLA Ops:
  6.5 79.1 %all-gather.2.cloned.1.call-start = ((), (), s32[]{:S(2)}) async-start(), calls=%async_computation | async-start | bytes 4718592 | tf_op jit(solution)/shard_map/all_gather | solution.py:31
  7.3 16.7 %copy-start.1 = (s32[20,256]{1,0:T(8,128)S(1)}, s32[20,256]{1,0:T(8,128)}, u32[]{:S(2)}) copy-start(s32[20,256]{1,0:T(8,128)} %param.7) | copy-start | bytes 61444
  7.3 16.7 %copy-start.2 = (s32[20,256]{1,0:T(8,128)S(1)}, s32[20,256]{1,0:T(8,128)}, u32[]{:S(2)}) copy-start(s32[20,256]{1,0:T(8,128)} %param.6) | copy-start | bytes 61444
  7.3 591.3 %all-reduce.4.cloned.1.call-start = ((), (), s32[]{:S(2)}) async-start(), calls=%async_computation.1 | async-start | bytes 8388608 | tf_op jit(solution)/shard_map/psum | solution.py:50
  266.9 66.9 %copy-start.3 = (s32[256]{0:T(256)S(1)}, s32[256]{0:T(256)}, u32[]{:S(2)}) copy-start(s32[256]{0:T(256)} %param.8) | copy-start | bytes 3076
  1130.6 173.1 %copy-start = (f32[1,131072]{1,0:T(1,128)S(1)}, f32[1,131072]{1,0:T(1,128)}, u32[]{:S(2)}) copy-start(f32[1,131072]{1,0:T(1,128)} %get-tuple-element.60) | copy-start | bytes 1572868
Sparse Core Ops, SparseCore 0:
  9.5 76.0 all-gather.1
  443.4 155.1 all-reduce.3
